TPU v7x, 32 devices: a whole 2x2x4 slice. The times are simulated.
32 devices in a mesh: dp: 8 (over y, x, core), ctx: 4 (over z).
Axes of the slice: x: 2, y: 2, z: 4, core: 2. Of those that a mesh axis runs over, the one named last changes fastest.
Arguments:
- layer_input: bfloat16 [4096, 768], P(('dp', 'ctx')), may hold values from -6 to 6
- lengths: int32 [8], P('dp'), may hold values from 128 to 512, as said below
- qkv_weight: bfloat16 [768, 2304], P(('dp', 'ctx')), may hold values from -1 to 1
- qv_bias: bfloat16 [1536], P(('dp', 'ctx')), may hold values from -3 to 3
- out_weight: bfloat16 [768, 768], P(('dp', 'ctx')), may hold values from -1.75 to 1.75
- out_bias: bfloat16 [768], P(('dp', 'ctx')), may hold values from -3 to 3
- first_gain: bfloat16 [768], P(('dp', 'ctx')), may hold values from 0.099609375 to 1.8984375
- first_shift: bfloat16 [768], P(('dp', 'ctx')), may hold values from -3 to 3
- up_weight: bfloat16 [768, 3072], P(('dp', 'ctx')), may hold values from -0.21875 to 0.21875
- up_bias: bfloat16 [3072], P(('dp', 'ctx')), may hold values from -3 to 3
- down_weight: bfloat16 [3072, 768], P(('dp', 'ctx')), may hold values from -0.109375 to 0.109375
- down_bias: bfloat16 [768], P(('dp', 'ctx')), may hold values from -3 to 3
- second_gain: bfloat16 [768], P(('dp', 'ctx')), may hold values from 0.099609375 to 1.8984375
- second_shift: bfloat16 [768], P(('dp', 'ctx')), may hold values from -3 to 3
- cotangent: bfloat16 [4096, 768], P(('dp', 'ctx')), may hold values from -6 to 6
Outputs:
- layer_output: bfloat16 [4096, 768], P(('dp', 'ctx'))
- input_grad: float32 [4096, 768], P(('dp', 'ctx'))
- qkv_weight_grad: float32 [768, 2304], P(('dp', 'ctx'))
- qv_bias_grad: float32 [1536], P(('dp', 'ctx'))
- out_weight_grad: float32 [768, 768], P(('dp', 'ctx'))
- out_bias_grad: float32 [768], P(('dp', 'ctx'))
- first_gain_grad: float32 [768], P(('dp', 'ctx'))
- first_shift_grad: float32 [768], P(('dp', 'ctx'))
- up_weight_grad: float32 [768, 3072], P(('dp', 'ctx'))
- up_bias_grad: float32 [3072], P(('dp', 'ctx'))
- down_weight_grad: float32 [3072, 768], P(('dp', 'ctx'))
- down_bias_grad: float32 [768], P(('dp', 'ctx'))
- second_gain_grad: float32 [768], P(('dp', 'ctx'))
- second_shift_grad: float32 [768], P(('dp', 'ctx'))
Inputs may be any that keep to these rules, and one draw needn't show every extreme that they name: `lengths`: each entry is one of the 512 positions or fewer, some sequence has all 512 valid.
All inputs are finite; a program needn't handle non-finite values.
Results may differ from a plain program's by a relative error of at most 0.014.
The roundings to bfloat16 on the way count: a program that leaves them out, or rounds other values in their place, can miss the bound.
Values may be sent and summed in bfloat16 or wider, within the bound.
A program may use at most 192 MiB of HBM per device.

v0:
```python
import jax
import jax.numpy as jnp
from jax import lax
from jax.sharding import PartitionSpec as P

HEAD_DIM = 64


EPSILON = 1e-05


def gelu_tanh(value):
    return (
        0.5
        * value
        * (1.0 + jnp.tanh(0.7978845608028654 * (value + 0.044715 * value * value * value)))
    )


def product(left, right):
    return jnp.dot(left, right, preferred_element_type=jnp.float32)


def product_tn(left, right):
    return lax.dot_general(
        left, right, (((0,), (0,)), ((), ())), preferred_element_type=jnp.float32
    )


def product_nt(left, right):
    return lax.dot_general(
        left, right, (((1,), (1,)), ((), ())), preferred_element_type=jnp.float32
    )


def norm_forward(rows, gain, shift):
    centered = rows - jnp.mean(rows, axis=-1, keepdims=True)
    inverse = lax.rsqrt(jnp.mean(centered * centered, axis=-1, keepdims=True) + EPSILON)
    normed = centered * inverse
    return (normed * gain + shift, normed, inverse)


def norm_backward(grad_rows, normed, inverse, gain):
    scaled = grad_rows * gain
    return inverse * (
        scaled
        - jnp.mean(scaled, axis=-1, keepdims=True)
        - normed * jnp.mean(scaled * normed, axis=-1, keepdims=True)
    )


def split_heads(array):
    return array.reshape(array.shape[0], 2, HEAD_DIM)


def pair_scores(query_pair, key_pair, key_valid):
    scores = jnp.einsum(
        "qhd,khd->hqk",
        split_heads(query_pair),
        split_heads(key_pair),
        preferred_element_type=jnp.float32,
    ) * HEAD_DIM ** (-0.5)
    return jnp.where(key_valid[None, None, :], scores, -jnp.inf)


def attention_forward(queries, keys_all, values_all, key_valid):
    outputs = []
    totals = []
    for pair_index in range(queries.shape[1] // (2 * HEAD_DIM)):
        offset = pair_index * 2 * HEAD_DIM
        columns = slice(offset, offset + 2 * HEAD_DIM)
        scores = pair_scores(queries[:, columns], keys_all[:, columns], key_valid)
        row_peak = jnp.max(scores, axis=-1, keepdims=True)
        log_total = row_peak + jnp.log(jnp.sum(jnp.exp(scores - row_peak), axis=-1, keepdims=True))
        attn_weights = jnp.exp(scores - log_total).astype(jnp.bfloat16)
        mixed_heads = jnp.einsum(
            "hqk,khd->qhd",
            attn_weights,
            split_heads(values_all[:, columns]),
            preferred_element_type=jnp.float32,
        )
        outputs.append(mixed_heads.reshape(mixed_heads.shape[0], 2 * HEAD_DIM))
        totals.append(log_total)
    return (jnp.concatenate(outputs, axis=1), totals)


def attention_query_side(queries, keys_all, values_all, key_valid, totals, grad_attended):
    grad_q_list = []
    inner_list = []
    for pair_index in range(queries.shape[1] // (2 * HEAD_DIM)):
        offset = pair_index * 2 * HEAD_DIM
        columns = slice(offset, offset + 2 * HEAD_DIM)
        scores = pair_scores(queries[:, columns], keys_all[:, columns], key_valid)
        probs = jnp.exp(scores - totals[pair_index])
        heads_grad = split_heads(grad_attended[:, columns])
        grad_probs = jnp.einsum(
            "qhd,khd->hqk",
            heads_grad,
            split_heads(values_all[:, columns]),
            preferred_element_type=jnp.float32,
        )
        inner = jnp.sum(probs * grad_probs, axis=-1, keepdims=True)
        grad_scores = probs * (grad_probs - inner)
        grad_low = grad_scores.astype(jnp.bfloat16)
        grad_queries = jnp.einsum(
            "hqk,khd->qhd",
            grad_low,
            split_heads(keys_all[:, columns]),
            preferred_element_type=jnp.float32,
        ) * HEAD_DIM ** (-0.5)
        grad_q_list.append(grad_queries.reshape(grad_queries.shape[0], 2 * HEAD_DIM))
        inner_list.append(inner)
    return (jnp.concatenate(grad_q_list, axis=1), inner_list)


def attention_key_side(
    all_queries, keys_local, values_local, local_valid, all_totals, all_inner, all_grad_att
):
    grad_k_list = []
    grad_v_list = []
    for pair_index in range(keys_local.shape[1] // (2 * HEAD_DIM)):
        offset = pair_index * 2 * HEAD_DIM
        columns = slice(offset, offset + 2 * HEAD_DIM)
        head_span = slice(2 * pair_index, 2 * pair_index + 2)
        scores = pair_scores(all_queries[:, columns], keys_local[:, columns], local_valid)
        probs = jnp.exp(scores - all_totals[:, head_span].T[:, :, None])
        probs_low = probs.astype(jnp.bfloat16)
        heads_grad = split_heads(all_grad_att[:, columns])
        grad_values = jnp.einsum(
            "hqk,qhd->khd", probs_low, heads_grad, preferred_element_type=jnp.float32
        )
        grad_probs = jnp.einsum(
            "qhd,khd->hqk",
            heads_grad,
            split_heads(values_local[:, columns]),
            preferred_element_type=jnp.float32,
        )
        grad_scores = probs * (grad_probs - all_inner[:, head_span].T[:, :, None])
        grad_low = grad_scores.astype(jnp.bfloat16)
        grad_keys = jnp.einsum(
            "hqk,qhd->khd",
            grad_low,
            split_heads(all_queries[:, columns]),
            preferred_element_type=jnp.float32,
        ) * HEAD_DIM ** (-0.5)
        grad_k_list.append(grad_keys.reshape(grad_keys.shape[0], 2 * HEAD_DIM))
        grad_v_list.append(grad_values.reshape(grad_values.shape[0], 2 * HEAD_DIM))
    return (jnp.concatenate(grad_k_list, axis=1), jnp.concatenate(grad_v_list, axis=1))


def stack_rows(pieces):
    return jnp.concatenate(pieces, axis=0)[:, :, 0].T


def on_device(
    layer_input,
    lengths,
    qkv_weight,
    qv_bias,
    out_weight,
    out_bias,
    first_gain,
    first_shift,
    up_weight,
    up_bias,
    down_weight,
    down_bias,
    second_gain,
    second_shift,
    cotangent,
):
    width = layer_input.shape[1]
    (
        full_qkv,
        full_qv_bias,
        full_out,
        full_out_bias,
        gain_first,
        shift_first,
        full_up,
        full_up_bias,
        full_down,
        full_down_bias,
        gain_second,
        shift_second,
    ) = (
        lax.all_gather(qkv_weight, ("dp", "ctx"), axis=0, tiled=True),
        lax.all_gather(qv_bias, ("dp", "ctx"), axis=0, tiled=True),
        lax.all_gather(out_weight, ("dp", "ctx"), axis=0, tiled=True),
        lax.all_gather(out_bias, ("dp", "ctx"), axis=0, tiled=True),
        lax.all_gather(first_gain, ("dp", "ctx"), axis=0, tiled=True),
        lax.all_gather(first_shift, ("dp", "ctx"), axis=0, tiled=True),
        lax.all_gather(up_weight, ("dp", "ctx"), axis=0, tiled=True),
        lax.all_gather(up_bias, ("dp", "ctx"), axis=0, tiled=True),
        lax.all_gather(down_weight, ("dp", "ctx"), axis=0, tiled=True),
        lax.all_gather(down_bias, ("dp", "ctx"), axis=0, tiled=True),
        lax.all_gather(second_gain, ("dp", "ctx"), axis=0, tiled=True),
        lax.all_gather(second_shift, ("dp", "ctx"), axis=0, tiled=True),
    )
    joined = product(layer_input, full_qkv)
    bias_wide = full_qv_bias.astype(jnp.float32)
    queries = (joined[:, :width] + bias_wide[:width]).astype(jnp.bfloat16)
    keys_local = joined[:, width : 2 * width].astype(jnp.bfloat16)
    values_local = (joined[:, 2 * width :] + bias_wide[width:]).astype(jnp.bfloat16)
    keys_all, values_all = (
        lax.all_gather(keys_local, "ctx", axis=0, tiled=True),
        lax.all_gather(values_local, "ctx", axis=0, tiled=True),
    )
    key_valid = jnp.arange(keys_all.shape[0], dtype=jnp.int32) < lengths[0]
    attended, totals = attention_forward(queries, keys_all, values_all, key_valid)
    attended_low = attended.astype(jnp.bfloat16)
    first_sum = (
        layer_input.astype(jnp.float32)
        + product(attended_low, full_out)
        + full_out_bias.astype(jnp.float32)
    )
    gain_one = gain_first.astype(jnp.float32)
    hidden, normed_first, inverse_first = norm_forward(
        first_sum, gain_one, shift_first.astype(jnp.float32)
    )
    hidden_low = hidden.astype(jnp.bfloat16)
    upper = product(hidden_low, full_up) + full_up_bias.astype(jnp.float32)
    activation, gelu_back = jax.vjp(gelu_tanh, upper)
    activation_low = activation.astype(jnp.bfloat16)
    second_sum = hidden + product(activation_low, full_down) + full_down_bias.astype(jnp.float32)
    gain_two = gain_second.astype(jnp.float32)
    result, normed_second, inverse_second = norm_forward(
        second_sum, gain_two, shift_second.astype(jnp.float32)
    )
    layer_output = result.astype(jnp.bfloat16)
    back_qkv, back_out, back_up, back_down = (full_qkv, full_out, full_up, full_down)
    cot_wide = cotangent.astype(jnp.float32)
    second_shift_grad = jnp.sum(cot_wide, axis=0)
    second_gain_grad = jnp.sum(cot_wide * normed_second, axis=0)
    grad_second = norm_backward(cot_wide, normed_second, inverse_second, gain_two)
    down_bias_grad = jnp.sum(grad_second, axis=0)
    grad_second_low = grad_second.astype(jnp.bfloat16)
    down_weight_grad = product_tn(activation_low, grad_second_low)
    grad_upper = gelu_back(product_nt(grad_second_low, back_down))[0]
    up_bias_grad = jnp.sum(grad_upper, axis=0)
    grad_upper_low = grad_upper.astype(jnp.bfloat16)
    up_weight_grad = product_tn(hidden_low, grad_upper_low)
    grad_hidden = grad_second + product_nt(grad_upper_low, back_up)
    first_shift_grad = jnp.sum(grad_hidden, axis=0)
    first_gain_grad = jnp.sum(grad_hidden * normed_first, axis=0)
    grad_first = norm_backward(grad_hidden, normed_first, inverse_first, gain_one)
    out_bias_grad = jnp.sum(grad_first, axis=0)
    grad_first_low = grad_first.astype(jnp.bfloat16)
    out_weight_grad = product_tn(attended_low, grad_first_low)
    grad_attended = product_nt(grad_first_low, back_out).astype(jnp.bfloat16)
    grad_queries, inner_list = attention_query_side(
        queries, keys_all, values_all, key_valid, totals, grad_attended
    )
    all_queries, all_grad_att = (
        lax.all_gather(queries, "ctx", axis=0, tiled=True),
        lax.all_gather(grad_attended, "ctx", axis=0, tiled=True),
    )
    all_totals, all_inner = (
        lax.all_gather(stack_rows(totals), "ctx", axis=0, tiled=True),
        lax.all_gather(stack_rows(inner_list), "ctx", axis=0, tiled=True),
    )
    local_rows = keys_local.shape[0]
    local_valid = (
        lax.axis_index("ctx") * local_rows + jnp.arange(local_rows, dtype=jnp.int32) < lengths[0]
    )
    grad_keys, grad_values = attention_key_side(
        all_queries, keys_local, values_local, local_valid, all_totals, all_inner, all_grad_att
    )
    qv_bias_grad = jnp.concatenate([jnp.sum(grad_queries, axis=0), jnp.sum(grad_values, axis=0)])
    grad_joined = jnp.concatenate([grad_queries, grad_keys, grad_values], axis=1).astype(
        jnp.bfloat16
    )
    qkv_weight_grad = product_tn(layer_input, grad_joined)
    input_grad = grad_first + product_nt(grad_joined, back_qkv)
    summed = (
        lax.psum_scatter(qkv_weight_grad, ("dp", "ctx"), scatter_dimension=0, tiled=True),
        lax.psum_scatter(qv_bias_grad, ("dp", "ctx"), scatter_dimension=0, tiled=True),
        lax.psum_scatter(out_weight_grad, ("dp", "ctx"), scatter_dimension=0, tiled=True),
        lax.psum_scatter(out_bias_grad, ("dp", "ctx"), scatter_dimension=0, tiled=True),
        lax.psum_scatter(first_gain_grad, ("dp", "ctx"), scatter_dimension=0, tiled=True),
        lax.psum_scatter(first_shift_grad, ("dp", "ctx"), scatter_dimension=0, tiled=True),
        lax.psum_scatter(up_weight_grad, ("dp", "ctx"), scatter_dimension=0, tiled=True),
        lax.psum_scatter(up_bias_grad, ("dp", "ctx"), scatter_dimension=0, tiled=True),
        lax.psum_scatter(down_weight_grad, ("dp", "ctx"), scatter_dimension=0, tiled=True),
        lax.psum_scatter(down_bias_grad, ("dp", "ctx"), scatter_dimension=0, tiled=True),
        lax.psum_scatter(second_gain_grad, ("dp", "ctx"), scatter_dimension=0, tiled=True),
        lax.psum_scatter(second_shift_grad, ("dp", "ctx"), scatter_dimension=0, tiled=True),
    )
    return (
        layer_output,
        input_grad,
        summed[0],
        summed[1],
        summed[2],
        summed[3],
        summed[4],
        summed[5],
        summed[6],
        summed[7],
        summed[8],
        summed[9],
        summed[10],
        summed[11],
    )


def solution(mesh):
    placed = (
        P(("dp", "ctx"), None),
        P("dp"),
        P(("dp", "ctx"), None),
        P(("dp", "ctx")),
        P(("dp", "ctx"), None),
        P(("dp", "ctx")),
        P(("dp", "ctx")),
        P(("dp", "ctx")),
        P(("dp", "ctx"), None),
        P(("dp", "ctx")),
        P(("dp", "ctx"), None),
        P(("dp", "ctx")),
        P(("dp", "ctx")),
        P(("dp", "ctx")),
        P(("dp", "ctx"), None),
    )
    return jax.shard_map(
        on_device,
        mesh=mesh,
        in_specs=placed,
        out_specs=(
            P(("dp", "ctx"), None),
            P(("dp", "ctx"), None),
            P(("dp", "ctx"), None),
            P(("dp", "ctx")),
            P(("dp", "ctx"), None),
            P(("dp", "ctx")),
            P(("dp", "ctx")),
            P(("dp", "ctx")),
            P(("dp", "ctx"), None),
            P(("dp", "ctx")),
            P(("dp", "ctx"), None),
            P(("dp", "ctx")),
            P(("dp", "ctx")),
            P(("dp", "ctx")),
        ),
        check_vma=False,
    )
```

profile of v0, /device:TPU:0, one launch (start us, length us, event | category | flops | bytes accessed | tf_op | source)
XLA Modules:
  0.0 860.1 jit_solution(4276560819131009977)
XLA Ops:
  16.8 42.4 %all-reduce.17 = (bf16[1536]{0:T(1024)(128)(2,1)S(1)}, bf16[768]{0:T(1024)(128)(2,1)S(1)}, bf16[768]{0:T(1024)(128)(2,1)S(1)}, bf16[768]{0:T(1024)(128)(2,1)S(1)...) all-reduce(bf16[1536]{0:T(1024)(128)(2,1)S(1)} %dynamic-update-slic, ...), channel_id=1, replica_groups=mesh['dp'=8,'ctx'=4] {'dp','ctx'}, use_global_device_ids=true, to_apply=%add | all-reduce | flops 9216 | bytes 36864
  62.8 11.0 %all-gather.5.cloned.1.call-done = bf16[768,2304]{1,0:T(8,128)(2,1)} async-done(((bf16[24,2304]{1,0:T(8,128)(2,1)}), bf16[768,2304]{1,0:T(8,128)(2,1)}) %all-gather.5.cloned.1.call-update) | async-done | bytes 3538960 | tf_op jit(solution)/shard_map/all_gather | solution.py:187
  73.8 2.8 fusion.145
  76.6 18.8 %all_gather.56 = bf16[512,768]{1,0:T(8,128)(2,1)S(1)} all-gather(bf16[128,768]{1,0:T(8,128)(2,1)S(1)} %get-tuple-element.85), channel_id=1, replica_groups=mesh['dp'=8,'ctx'=4] {'ctx'}, dimensions={0}, use_global_device_ids=true | all-gather | bytes 983040 | tf_op jit(solution)/shard_map/all_gather | solution.py:207
  95.5 19.5 %all_gather.68 = bf16[512,768]{1,0:T(8,128)(2,1)S(1)} all-gather(bf16[128,768]{1,0:T(8,128)(2,1)S(1)} %get-tuple-element.84), channel_id=1, replica_groups=mesh['dp'=8,'ctx'=4] {'ctx'}, dimensions={0}, use_global_device_ids=true | all-gather | bytes 983040 | tf_op jit(solution)/shard_map/all_gather | solution.py:255
  116.6 19.8 %all_gather.57 = bf16[512,768]{1,0:T(8,128)(2,1)S(1)} all-gather(bf16[128,768]{1,0:T(8,128)(2,1)S(1)} %slice.303), channel_id=1, replica_groups=mesh['dp'=8,'ctx'=4] {'ctx'}, dimensions={0}, use_global_device_ids=true | all-gather | bytes 983040 | tf_op jit(solution)/shard_map/all_gather | solution.py:206
  162.9 2.6 concatenate.25
  165.4 14.3 %all_gather.69 = f32[512,12]{0,1:T(8,128)} all-gather(f32[128,12]{0,1:T(8,128)} %bitcast.361), channel_id=1, replica_groups=mesh['dp'=8,'ctx'=4] {'ctx'}, dimensions={0}, use_global_device_ids=true | all-gather | bytes 30720 | tf_op jit(solution)/shard_map/all_gather | solution.py:259
  187.7 1.9 fusion.152
  191.3 2.1 fusion.22
  199.1 4.4 convolution_add_fusion
  203.5 57.8 %all-gather.11.cloned.1.call-done = bf16[3072,768]{1,0:T(8,128)(2,1)} async-done(((bf16[96,768]{1,0:T(8,128)(2,1)}), bf16[3072,768]{1,0:T(8,128)(2,1)}) %all-gather.11.cloned.1.call-update) | async-done | bytes 4718608 | tf_op jit(solution)/shard_map/all_gather | solution.py:195
  261.2 4.1 fusion.153
  266.4 1.5 fusion.133
  267.9 3.0 fusion.154
  270.9 2.3 multiply_reduce_fusion.6
  275.8 19.0 %all_gather.70 = bf16[512,768]{1,0:T(8,128)(2,1)} all-gather(bf16[128,768]{1,0:T(8,128)(2,1)S(1)} %convolution_convert_fusion), channel_id=1, replica_groups=mesh['dp'=8,'ctx'=4] {'ctx'}, dimensions={0}, use_global_device_ids=true | all-gather | bytes 983040 | tf_op jit(solution)/shard_map/all_gather | solution.py:256
  294.7 2.8 fusion.122
  297.5 1.5 copy.157
  302.7 1.5 copy.158
  304.2 1.8 multiply_reduce_fusion.4
  306.0 1.5 copy.159
  307.5 2.5 multiply_reduce_fusion.3
  311.4 2.6 multiply_reduce_fusion.2
  314.0 1.5 copy.161
  315.5 2.5 multiply_reduce_fusion.1
  319.5 2.6 multiply_reduce_fusion
  323.0 1.7 copy.165
  324.7 2.0 convolution_multiply_fusion.16
  328.1 1.7 convolution_multiply_fusion.14
  331.3 13.1 %all_gather.71 = f32[512,12]{0,1:T(8,128)S(1)} all-gather(f32[128,12]{0,1:T(8,128)S(1)} %bitcast.360), channel_id=1, replica_groups=mesh['dp'=8,'ctx'=4] {'ctx'}, dimensions={0}, use_global_device_ids=true | all-gather | bytes 30720 | tf_op jit(solution)/shard_map/all_gather | solution.py:260
  348.2 2.1 fusion.55
  351.1 2.0 fusion.56
  354.0 2.0 fusion.57
  356.8 2.0 fusion.58
  359.5 2.0 fusion.59
  361.5 2.0 fusion.60
  368.2 3.9 convolution_bitcast_fusion
  372.1 8.2 copy.188
  381.4 5.2 fusion.76
  388.1 5.2 fusion.125
  393.3 1.6 constant_dynamic-update-slice_fusion.35
  403.5 1.5 constant_dynamic-update-slice_fusion.29
  413.5 39.8 %all-reduce.16 = (f32[1536]{0:T(1024)S(1)}, f32[768]{0:T(1024)}, f32[768]{0:T(1024)}, f32[768]{0:T(1024)}, f32[3072]{0:T(1024)}, /*index=5*/f32[768]{0:T(1024)}, f32[768]{0:T(1024)}, f32[768]{0:T(1024)}) all-reduce(f32[1536]{0:T(1024)S(1)} %pad_maximum_fusion, ...), channel_id=3, replica_groups=mesh['dp'=8,'ctx'=4] {'dp','ctx'}, use_global_device_ids=true, to_apply=%region_29.30.clone | all-reduce | flops 9216 | bytes 73728
  462.6 3.2 convolution_add_fusion.2
  465.9 104.2 %reduce-scatter.13.cloned.1.call-done = f32[24,2304]{1,0:T(8,128)} async-done(((f32[768,2304]{1,0:T(8,128)}), f32[24,2304]{1,0:T(8,128)}) %reduce-scatter.13.cloned.1.call-update) | async-done | bytes 221200
  570.0 141.6 %reduce-scatter.9.cloned.1.call-done = f32[24,3072]{1,0:T(8,128)} async-done(((f32[768,3072]{1,0:T(8,128)}), f32[24,3072]{1,0:T(8,128)}) %reduce-scatter.9.cloned.1.call-update) | async-done | bytes 294928 | tf_op jit(solution)/shard_map/reduce_scatter | solution.py:282
  711.6 141.7 %reduce-scatter.11.cloned.1.call-done = f32[96,768]{1,0:T(8,128)} async-done(((f32[3072,768]{1,0:T(8,128)}), f32[96,768]{1,0:T(8,128)}) %reduce-scatter.11.cloned.1.call-update) | async-done | bytes 294928 | tf_op jit(solution)/shard_map/reduce_scatter | solution.py:284
  (379 shorter events, 109.8 us)
Async XLA Ops:
  7.2 66.6 %all-gather.5.cloned.1.call-start = ((), (), s32[]{:S(2)}) async-start(), calls=%async_computation.4 | async-start | bytes 3649536 | tf_op jit(solution)/shard_map/all_gather | solution.py:187
  7.9 179.8 %all-gather.7.cloned.1.call-start = ((), (), s32[]{:S(2)}) async-start(), calls=%async_computation.5 | async-start | bytes 1216512 | tf_op jit(solution)/shard_map/all_gather | solution.py:189
  8.7 190.4 %all-gather.9.cloned.1.call-start = ((), (), s32[]{:S(2)}) async-start(), calls=%async_computation.6 | async-start | bytes 4866048 | tf_op jit(solution)/shard_map/all_gather | solution.py:193
  9.4 251.8 %all-gather.11.cloned.1.call-start = ((), (), s32[]{:S(2)}) async-start(), calls=%async_computation.7 | async-start | bytes 4866048 | tf_op jit(solution)/shard_map/all_gather | solution.py:195
  10.0 455.9 %reduce-scatter.7.cloned.1.call-start = ((), (), s32[]{:S(2)}) async-start(), calls=%async_computation.8 | async-start | bytes 2433024 | tf_op jit(solution)/shard_map/reduce_scatter | solution.py:278
  136.7 19.8 %copy-start.36 = (bf16[512,128]{0,1:T(8,128)(2,1)}, bf16[512,128]{0,1:T(8,128)(2,1)S(1)}, u32[]{:S(2)}) copy-start(bf16[512,128]{0,1:T(8,128)(2,1)S(1)} %copy.141) | copy-start | bytes 393220
  137.7 19.4 %copy-start.23 = (bf16[512,128]{0,1:T(8,128)(2,1)}, bf16[512,128]{0,1:T(8,128)(2,1)S(1)}, u32[]{:S(2)}) copy-start(bf16[512,128]{0,1:T(8,128)(2,1)S(1)} %copy.144) | copy-start | bytes 393220
  138.7 18.9 %copy-start.24 = (bf16[512,128]{0,1:T(8,128)(2,1)}, bf16[512,128]{0,1:T(8,128)(2,1)S(1)}, u32[]{:S(2)}) copy-start(bf16[512,128]{0,1:T(8,128)(2,1)S(1)} %copy.147) | copy-start | bytes 393220
  139.8 18.5 %copy-start.25 = (bf16[512,128]{0,1:T(8,128)(2,1)}, bf16[512,128]{0,1:T(8,128)(2,1)S(1)}, u32[]{:S(2)}) copy-start(bf16[512,128]{0,1:T(8,128)(2,1)S(1)} %copy.150) | copy-start | bytes 393220
  140.8 18.0 %copy-start.27 = (bf16[512,128]{0,1:T(8,128)(2,1)}, bf16[512,128]{0,1:T(8,128)(2,1)S(1)}, u32[]{:S(2)}) copy-start(bf16[512,128]{0,1:T(8,128)(2,1)S(1)} %copy.153) | copy-start | bytes 393220
  143.2 13.3 %copy-start.61 = (bf16[128,128]{0,1:T(8,128)(2,1)S(1)}, bf16[128,128]{0,1:T(8,128)(2,1)}, u32[]{:S(2)}) copy-start(bf16[128,128]{0,1:T(8,128)(2,1)} %copy.140) | copy-start | bytes 98308
  158.6 21.2 %copy-start.31 = (bf16[512,128]{0,1:T(8,128)(2,1)S(1)}, bf16[512,128]{0,1:T(8,128)(2,1)}, u32[]{:S(2)}) copy-start(bf16[512,128]{0,1:T(8,128)(2,1)} %copy.139) | copy-start | bytes 393220
  159.8 25.0 %copy-start.34 = (bf16[512,128]{0,1:T(8,128)(2,1)S(1)}, bf16[512,128]{0,1:T(8,128)(2,1)}, u32[]{:S(2)}) copy-start(bf16[512,128]{0,1:T(8,128)(2,1)} %copy.148) | copy-start | bytes 393220
  160.0 25.8 %copy-start.33 = (bf16[512,128]{0,1:T(8,128)(2,1)S(1)}, bf16[512,128]{0,1:T(8,128)(2,1)}, u32[]{:S(2)}) copy-start(bf16[512,128]{0,1:T(8,128)(2,1)} %copy.151) | copy-start | bytes 393220
  165.4 17.8 %copy-start.35 = (bf16[512,128]{0,1:T(8,128)(2,1)S(1)}, bf16[512,128]{0,1:T(8,128)(2,1)}, u32[]{:S(2)}) copy-start(bf16[512,128]{0,1:T(8,128)(2,1)} %copy.145) | copy-start | bytes 393220
  165.4 19.4 %copy-start.70 = (f32[2,128]{1,0:T(2,128)S(1)}, f32[2,128]{1,0:T(2,128)}, u32[]{:S(2)}) copy-start(f32[2,128]{1,0:T(2,128)} %log_add_fusion.2) | copy-start | bytes 3076
  165.4 20.3 %copy-start.68 = (f32[2,128]{1,0:T(2,128)S(1)}, f32[2,128]{1,0:T(2,128)}, u32[]{:S(2)}) copy-start(f32[2,128]{1,0:T(2,128)} %log_add_fusion.1) | copy-start | bytes 3076
  180.7 6.0 copy-start.32
  187.7 5.7 copy-start.60
  187.7 5.7 copy-start.63
  187.7 5.7 copy-start.87
  187.7 6.9 copy-start.58
  187.7 6.9 copy-start.64
  189.6 6.1 copy-start.57
  189.6 6.1 copy-start.65
  191.3 5.5 copy-start.56
  191.3 5.5 copy-start.66
  261.2 5.1 copy-start.75
  261.2 6.6 copy-start.86
  274.0 20.7 %copy-start.3 = (f32[128,768]{1,0:T(8,128)}, f32[128,768]{1,0:T(8,128)S(1)}, u32[]{:S(2)}) copy-start(f32[128,768]{1,0:T(8,128)S(1)} %get-tuple-element.83) | copy-start | bytes 1179652
  297.5 6.7 copy-start.71
  306.0 9.5 %copy-start.69 = (f32[2,128]{1,0:T(2,128)S(1)}, f32[2,128]{1,0:T(2,128)}, u32[]{:S(2)}) copy-start(f32[2,128]{1,0:T(2,128)} %log_add_fusion.1) | copy-start | bytes 3076
  328.0 19.7 %copy-start.41 = (f32[2,64,128]{2,1,0:T(8,128)}, f32[2,64,128]{2,1,0:T(8,128)S(1)}, u32[]{:S(2)}) copy-start(f32[2,64,128]{2,1,0:T(8,128)S(1)} %convolution_multiply_fusion.15) | copy-start | bytes 196612
  329.8 15.2 %copy-start.55 = (bf16[512,128]{1,0:T(8,128)(2,1)S(1)}, bf16[512,128]{1,0:T(8,128)(2,1)}, u32[]{:S(2)}) copy-start(bf16[512,128]{1,0:T(8,128)(2,1)} %get-tuple-element.90) | copy-start | bytes 393220
  329.8 16.0 %copy-start.54 = (bf16[512,128]{1,0:T(8,128)(2,1)S(1)}, bf16[512,128]{1,0:T(8,128)(2,1)}, u32[]{:S(2)}) copy-start(bf16[512,128]{1,0:T(8,128)(2,1)} %get-tuple-element.89) | copy-start | bytes 393220
  329.8 16.8 %copy-start.53 = (bf16[512,128]{1,0:T(8,128)(2,1)S(1)}, bf16[512,128]{1,0:T(8,128)(2,1)}, u32[]{:S(2)}) copy-start(bf16[512,128]{1,0:T(8,128)(2,1)} %get-tuple-element.88) | copy-start | bytes 393220
  329.9 16.9 %copy-start.52 = (bf16[512,128]{1,0:T(8,128)(2,1)S(1)}, bf16[512,128]{1,0:T(8,128)(2,1)}, u32[]{:S(2)}) copy-start(bf16[512,128]{1,0:T(8,128)(2,1)} %get-tuple-element.87) | copy-start | bytes 393220
  329.9 17.0 %copy-start.51 = (bf16[512,128]{1,0:T(8,128)(2,1)S(1)}, bf16[512,128]{1,0:T(8,128)(2,1)}, u32[]{:S(2)}) copy-start(bf16[512,128]{1,0:T(8,128)(2,1)} %get-tuple-element.86) | copy-start | bytes 393220
  331.2 16.6 %copy-start.44 = (f32[2,64,128]{2,1,0:T(8,128)}, f32[2,64,128]{2,1,0:T(8,128)S(1)}, u32[]{:S(2)}) copy-start(f32[2,64,128]{2,1,0:T(8,128)S(1)} %convolution_multiply_fusion.12) | copy-start | bytes 196612
  347.1 6.9 copy-start.19
  347.1 222.9 %reduce-scatter.13.cloned.1.call-start = ((), (), s32[]{:S(2)}) async-start(), calls=%async_computation.11 | async-start | bytes 7299072
  348.2 16.8 %copy-start.45 = (f32[2,64,128]{2,1,0:T(8,128)}, f32[2,64,128]{2,1,0:T(8,128)S(1)}, u32[]{:S(2)}) copy-start(f32[2,64,128]{2,1,0:T(8,128)S(1)} %fusion.96) | copy-start | bytes 196612
  348.2 8.6 copy-start.18
  350.3 9.2 %copy-start.17 = (f32[2,512,128]{2,1,0:T(8,128)S(1)}, f32[2,512,128]{2,1,0:T(8,128)}, u32[]{:S(2)}) copy-start(f32[2,512,128]{2,1,0:T(8,128)} %fusion.10) | copy-start | bytes 1572868
  353.1 8.3 copy-start.16
  380.3 331.3 %reduce-scatter.9.cloned.1.call-start = ((), (), s32[]{:S(2)}) async-start(), calls=%async_computation.9 | async-start | bytes 9732096 | tf_op jit(solution)/shard_map/reduce_scatter | solution.py:282
  386.6 466.7 %reduce-scatter.11.cloned.1.call-start = ((), (), s32[]{:S(2)}) async-start(), calls=%async_computation.10 | async-start | bytes 9732096 | tf_op jit(solution)/shard_map/reduce_scatter | solution.py:284
  393.3 69.4 %copy-start = (bf16[768,2304]{1,0:T(8,128)(2,1)S(1)}, bf16[768,2304]{1,0:T(8,128)(2,1)}, u32[]{:S(2)}) copy-start(bf16[768,2304]{1,0:T(8,128)(2,1)} %all-gather.5.cloned.1.call-done) | copy-start | bytes 10616836
  (50 other events, 138.2 us)
Sparse Core Ops, SparseCore 0:
  10.8 62.9 all-gather.4
  76.6 54.1 all-gather.6
  133.6 62.9 all-gather.8
  199.2 61.9 all-gather.10
  347.2 98.0 reduce-scatter.6
  451.4 118.5 reduce-scatter.12
  576.5 135.0 reduce-scatter.8
  718.1 135.1 reduce-scatter.10
where the time goes:
time: 863 us; the launch traced here: 860 us
  waiting for transfers between devices  459 us (53%)
  blocking collectives  187 us (22%)
  local copies, waits for them, and re-layouts  94.9 us (11%)
  matrix products  89.2 us (10%)
  between operations  15.9 us (2%)
  other arithmetic  14.2 us (2%)
    reduce_scatter x1, waiting for transfers between devices, on_device(): lax.psum_scatter(down_weight_grad, ('dp', 'ctx'), scatter_dimension=0, ti...  142 us
    reduce_scatter x1, waiting for transfers between devices, on_device(): lax.psum_scatter(up_weight_grad, ('dp', 'ctx'), scatter_dimension=0, tile...  142 us
    unnamed x9, waiting for transfers between devices  107 us
    unnamed x2, blocking collectives  82.2 us
    all_gather x1, waiting for transfers between devices, on_device(): lax.all_gather(down_weight, ('dp', 'ctx'), axis=0, tiled=True)  57.8 us
    unnamed x226, local copies, waits for them, and re-layouts  51.6 us
    all_gather x1, blocking collectives, on_device(): lax.all_gather(keys_local, 'ctx', axis=0, tiled=True)  19.8 us
    all_gather x1, blocking collectives, on_device(): lax.all_gather(queries, 'ctx', axis=0, tiled=True)  19.5 us
  transfers between devices with their start and end apart: 8, of which 5 were waited for; matrix products, arithmetic and copies ran while one was open for 16% of the time, Pallas kernels for 0%

commit v1 on v0

v1 whole, which is shorter than its diff:
```python
import jax
import jax.numpy as jnp
from jax import lax
from jax.experimental import pallas as pl
from jax.experimental.pallas import tpu as pltpu
from jax.sharding import PartitionSpec as P

HEAD_DIM = 64


EPSILON = 1e-05


def gelu_tanh(value):
    return (
        0.5
        * value
        * (1.0 + jnp.tanh(0.7978845608028654 * (value + 0.044715 * value * value * value)))
    )


def product(left, right):
    return jnp.dot(left, right, preferred_element_type=jnp.float32)


def product_tn(left, right):
    return lax.dot_general(
        left, right, (((0,), (0,)), ((), ())), preferred_element_type=jnp.float32
    )


def product_nt(left, right):
    return lax.dot_general(
        left, right, (((1,), (1,)), ((), ())), preferred_element_type=jnp.float32
    )


def norm_forward(rows, gain, shift):
    centered = rows - jnp.mean(rows, axis=-1, keepdims=True)
    inverse = lax.rsqrt(jnp.mean(centered * centered, axis=-1, keepdims=True) + EPSILON)
    normed = centered * inverse
    return (normed * gain + shift, normed, inverse)


def norm_backward(grad_rows, normed, inverse, gain):
    scaled = grad_rows * gain
    return inverse * (
        scaled
        - jnp.mean(scaled, axis=-1, keepdims=True)
        - normed * jnp.mean(scaled * normed, axis=-1, keepdims=True)
    )


LANES = 128
AXES = ("dp", "ctx")


def head_scores(query, key, limit):
    scores = product_nt(query, key) * HEAD_DIM ** (-0.5)
    position = lax.broadcasted_iota(jnp.int32, scores.shape, 1)
    return jnp.where(position < limit, scores, -jnp.inf)


def log_sum(scores):
    peak = jnp.max(scores, axis=-1, keepdims=True)
    return peak + jnp.log(jnp.sum(jnp.exp(scores - peak), axis=-1, keepdims=True))


def forward_kernel(length_ref, query_ref, key_ref, value_ref, out_ref):
    limit = length_ref[0]
    for head in range(LANES // HEAD_DIM):
        span = slice(head * HEAD_DIM, (head + 1) * HEAD_DIM)
        scores = head_scores(query_ref[:, span], key_ref[:, span], limit)
        weights = jnp.exp(scores - log_sum(scores)).astype(jnp.bfloat16)
        out_ref[:, span] = product(weights, value_ref[:, span]).astype(jnp.bfloat16)


def backward_kernel(
    length_ref, query_ref, key_ref, value_ref, grad_ref, gq_ref, gk_ref, gv_ref, qsum_ref, vsum_ref
):
    limit = length_ref[0]
    scale = HEAD_DIM ** (-0.5)
    for head in range(LANES // HEAD_DIM):
        span = slice(head * HEAD_DIM, (head + 1) * HEAD_DIM)
        query, key, value = query_ref[:, span], key_ref[:, span], value_ref[:, span]
        grad = grad_ref[:, span]
        scores = head_scores(query, key, limit)
        probs = jnp.exp(scores - log_sum(scores))
        grad_probs = product_nt(grad, value)
        inner = jnp.sum(probs * grad_probs, axis=-1, keepdims=True)
        grad_low = (probs * (grad_probs - inner)).astype(jnp.bfloat16)
        grad_query = product(grad_low, key) * scale
        gq_ref[:, span] = grad_query.astype(jnp.bfloat16)
        gk_ref[:, span] = (product_tn(grad_low, query) * scale).astype(jnp.bfloat16)
        grad_value = product_tn(probs.astype(jnp.bfloat16), grad)
        gv_ref[:, span] = grad_value.astype(jnp.bfloat16)
        qsum_ref[:, span] = jnp.broadcast_to(
            jnp.sum(grad_query, axis=0, keepdims=True), (8, HEAD_DIM)
        )
        vsum_ref[:, span] = jnp.broadcast_to(
            jnp.sum(grad_value, axis=0, keepdims=True), (8, HEAD_DIM)
        )


def attention_specs(rows, total, pairs):
    local = pl.BlockSpec((rows, LANES), lambda p: (0, p))
    return (
        pl.BlockSpec(memory_space=pltpu.SMEM),
        local,
        pl.BlockSpec((total, LANES), lambda p: (0, p)),
        pl.BlockSpec((total, LANES), lambda p: (0, pairs + p)),
    )


def attention_forward(lengths, queries, keys_values):
    rows, width = queries.shape
    total, pairs = keys_values.shape[0], width // LANES
    work = 4 * rows * total * width
    return pl.pallas_call(
        forward_kernel,
        grid=(pairs,),
        in_specs=attention_specs(rows, total, pairs),
        out_specs=pl.BlockSpec((rows, LANES), lambda p: (0, p)),
        out_shape=jax.ShapeDtypeStruct((rows, width), jnp.bfloat16),
        cost_estimate=pl.CostEstimate(
            flops=work, bytes_accessed=4 * total * width, transcendentals=work // 64
        ),
        name="attend_forward",
    )(lengths, queries, keys_values, keys_values)


def attention_backward(lengths, queries, keys_values, grad_attended):
    rows, width = queries.shape
    total, pairs = keys_values.shape[0], width // LANES
    work = 10 * rows * total * width
    local = pl.BlockSpec((rows, LANES), lambda p: (0, p))
    long = pl.BlockSpec((total, LANES), lambda p: (0, p))
    short = pl.BlockSpec((8, LANES), lambda p: (0, p))
    return pl.pallas_call(
        backward_kernel,
        grid=(pairs,),
        in_specs=(*attention_specs(rows, total, pairs), local),
        out_specs=(local, long, long, short, short),
        out_shape=(
            jax.ShapeDtypeStruct((rows, width), jnp.bfloat16),
            jax.ShapeDtypeStruct((total, width), jnp.bfloat16),
            jax.ShapeDtypeStruct((total, width), jnp.bfloat16),
            jax.ShapeDtypeStruct((8, width), jnp.float32),
            jax.ShapeDtypeStruct((8, width), jnp.float32),
        ),
        cost_estimate=pl.CostEstimate(
            flops=work, bytes_accessed=8 * total * width, transcendentals=work // 320
        ),
        name="attend_backward",
    )(lengths, queries, keys_values, keys_values, grad_attended)


def gather_all(array):
    return lax.all_gather(array, AXES, axis=0, tiled=True)


def gather_vectors(vectors):
    packed = jnp.concatenate([vector.astype(jnp.float32) for vector in vectors])
    padded = jnp.pad(packed, (0, -packed.shape[0] % (8 * LANES)))
    every = gather_all(padded.reshape(-1, LANES)).reshape(-1, padded.shape[0])
    spread, offset = [], 0
    for vector in vectors:
        spread.append(every[:, offset : offset + vector.shape[0]].reshape(-1))
        offset += vector.shape[0]
    return spread


def scatter_vectors(vectors, count):
    sizes = [vector.shape[0] // count for vector in vectors]
    packed = jnp.concatenate(
        [vector.reshape(count, size) for vector, size in zip(vectors, sizes)], axis=1
    )
    padded = jnp.pad(packed, ((0, 0), (0, -packed.shape[1] % (8 * LANES))))
    mine = lax.psum_scatter(
        padded.reshape(-1, LANES), AXES, scatter_dimension=0, tiled=True
    ).reshape(-1)
    pieces, offset = [], 0
    for size in sizes:
        pieces.append(mine[offset : offset + size])
        offset += size
    return pieces


def scatter_weight(grad):
    return lax.psum_scatter(
        grad.astype(jnp.bfloat16), AXES, scatter_dimension=0, tiled=True
    ).astype(jnp.float32)


def on_device(
    layer_input,
    lengths,
    qkv_weight,
    qv_bias,
    out_weight,
    out_bias,
    first_gain,
    first_shift,
    up_weight,
    up_bias,
    down_weight,
    down_bias,
    second_gain,
    second_shift,
    cotangent,
):
    width = layer_input.shape[1]
    count = lax.axis_size("dp") * lax.axis_size("ctx")
    (
        bias_wide,
        out_bias_wide,
        gain_one,
        shift_one,
        up_bias_wide,
        down_bias_wide,
        gain_two,
        shift_two,
    ) = gather_vectors(
        (qv_bias, out_bias, first_gain, first_shift, up_bias, down_bias, second_gain, second_shift)
    )
    sequence = lax.all_gather(layer_input, "ctx", axis=0, tiled=True)
    full_qkv = gather_all(qkv_weight)
    full_out = gather_all(out_weight)
    full_up = gather_all(up_weight)
    full_down = gather_all(down_weight)
    weight_q = full_qkv[:, :width]
    weight_k = full_qkv[:, width : 2 * width]
    weight_v = full_qkv[:, 2 * width :]
    queries = (product(layer_input, weight_q) + bias_wide[:width]).astype(jnp.bfloat16)
    kv_bias = jnp.concatenate([jnp.zeros((width,), jnp.float32), bias_wide[width:]])
    keys_values = (product(sequence, full_qkv[:, width:]) + kv_bias).astype(jnp.bfloat16)
    attended_low = attention_forward(lengths, queries, keys_values)
    first_sum = layer_input.astype(jnp.float32) + product(attended_low, full_out) + out_bias_wide
    hidden, normed_first, inverse_first = norm_forward(first_sum, gain_one, shift_one)
    hidden_low = hidden.astype(jnp.bfloat16)
    upper = product(hidden_low, full_up) + up_bias_wide
    activation, gelu_back = jax.vjp(gelu_tanh, upper)
    activation_low = activation.astype(jnp.bfloat16)
    second_sum = hidden + product(activation_low, full_down) + down_bias_wide
    result, normed_second, inverse_second = norm_forward(second_sum, gain_two, shift_two)
    layer_output = result.astype(jnp.bfloat16)
    cot_wide = cotangent.astype(jnp.float32)
    second_shift_grad = jnp.sum(cot_wide, axis=0)
    second_gain_grad = jnp.sum(cot_wide * normed_second, axis=0)
    grad_second = norm_backward(cot_wide, normed_second, inverse_second, gain_two)
    down_bias_grad = jnp.sum(grad_second, axis=0)
    grad_second_low = grad_second.astype(jnp.bfloat16)
    down_weight_grad = scatter_weight(product_tn(activation_low, grad_second_low))
    grad_upper = gelu_back(product_nt(grad_second_low, full_down))[0]
    up_bias_grad = jnp.sum(grad_upper, axis=0)
    grad_upper_low = grad_upper.astype(jnp.bfloat16)
    up_weight_grad = scatter_weight(product_tn(hidden_low, grad_upper_low))
    grad_hidden = grad_second + product_nt(grad_upper_low, full_up)
    first_shift_grad = jnp.sum(grad_hidden, axis=0)
    first_gain_grad = jnp.sum(grad_hidden * normed_first, axis=0)
    grad_first = norm_backward(grad_hidden, normed_first, inverse_first, gain_one)
    out_bias_grad = jnp.sum(grad_first, axis=0)
    grad_first_low = grad_first.astype(jnp.bfloat16)
    out_weight_grad = scatter_weight(product_tn(attended_low, grad_first_low))
    grad_attended = product_nt(grad_first_low, full_out).astype(jnp.bfloat16)
    grad_queries, grad_keys, grad_values, query_sums, value_sums = attention_backward(
        lengths, queries, keys_values, grad_attended
    )
    qv_bias_grad = jnp.concatenate([query_sums[0], value_sums[0]])
    input_share = product_nt(grad_keys, weight_k) + product_nt(grad_values, weight_v)
    others = lax.psum_scatter(
        input_share.astype(jnp.bfloat16), "ctx", scatter_dimension=0, tiled=True
    ).astype(jnp.float32)
    qkv_weight_grad = scatter_weight(
        jnp.concatenate(
            [
                product_tn(layer_input, grad_queries),
                product_tn(sequence, grad_keys),
                product_tn(sequence, grad_values),
            ],
            axis=1,
        )
    )
    input_grad = grad_first + product_nt(grad_queries, weight_q) + others
    (
        qv_bias_grad,
        out_bias_grad,
        first_gain_grad,
        first_shift_grad,
        up_bias_grad,
        down_bias_grad,
        second_gain_grad,
        second_shift_grad,
    ) = scatter_vectors(
        (
            qv_bias_grad,
            out_bias_grad,
            first_gain_grad,
            first_shift_grad,
            up_bias_grad,
            down_bias_grad,
            second_gain_grad,
            second_shift_grad,
        ),
        count,
    )
    return (
        layer_output,
        input_grad,
        qkv_weight_grad,
        qv_bias_grad,
        out_weight_grad,
        out_bias_grad,
        first_gain_grad,
        first_shift_grad,
        up_weight_grad,
        up_bias_grad,
        down_weight_grad,
        down_bias_grad,
        second_gain_grad,
        second_shift_grad,
    )


def solution(mesh):
    placed = (
        P(("dp", "ctx"), None),
        P("dp"),
        P(("dp", "ctx"), None),
        P(("dp", "ctx")),
        P(("dp", "ctx"), None),
        P(("dp", "ctx")),
        P(("dp", "ctx")),
        P(("dp", "ctx")),
        P(("dp", "ctx"), None),
        P(("dp", "ctx")),
        P(("dp", "ctx"), None),
        P(("dp", "ctx")),
        P(("dp", "ctx")),
        P(("dp", "ctx")),
        P(("dp", "ctx"), None),
    )
    return jax.shard_map(
        on_device,
        mesh=mesh,
        in_specs=placed,
        out_specs=(
            P(("dp", "ctx"), None),
            P(("dp", "ctx"), None),
            P(("dp", "ctx"), None),
            P(("dp", "ctx")),
            P(("dp", "ctx"), None),
            P(("dp", "ctx")),
            P(("dp", "ctx")),
            P(("dp", "ctx")),
            P(("dp", "ctx"), None),
            P(("dp", "ctx")),
            P(("dp", "ctx"), None),
            P(("dp", "ctx")),
            P(("dp", "ctx")),
            P(("dp", "ctx")),
        ),
        check_vma=False,
    )
```

time: 863 us -> 896 us (1.038)
  waiting for transfers between devices: 459 us -> 679 us
  blocking collectives: 187 us -> 88.9 us
  local copies, waits for them, and re-layouts: 94.9 us -> 37.1 us
  matrix products: 89.2 us -> 43 us
  Pallas kernels: 0 us -> 18.6 us
    unnamed x9 -> x12, waiting for transfers between devices: 107 us -> 203 us
    unnamed x2 -> x0, blocking collectives: 82.2 us -> none
    all_gather x4, waiting for transfers between devices: 68.8 us -> 134 us  [gather_all(): return lax.all_gather(array, AXES, axis=0, tiled=True)]
    reduce_scatter x3 -> x4, waiting for transfers between devices: 283 us -> 342 us  [the longest x3 319 us: scatter_weight(): lax.psum_scatter(grad.astype(jnp.bfloat16), AXES, scatter_dimension=0, ti...]
    dot_general x42 -> x0, matrix products: 49.9 us -> none  [the longest x6 13.3 us: attention_query_side(): jnp.einsum('qhd,khd->hqk', heads_grad, split_heads(values_all[:, columns]...]
    unnamed x226 -> x35, local copies, waits for them, and re-layouts: 51.6 us -> 9.42 us
    slice x57 -> x9, local copies, waits for them, and re-layouts: 35.7 us -> 4.62 us  [the longest x2 2.68 us: on_device(): qv_bias_grad = jnp.concatenate([query_sums[0], value_sums[0]])]
    pallas_call x0 -> x2, Pallas kernels: none -> 18.6 us  [the longest x1 10.8 us: attention_backward(): pl.pallas_call(backward_kernel, grid=(pairs,), in_specs=(*attention_specs...]
  transfers between devices with their start and end apart: 8 -> 10, of which waited for: 5 -> 9; matrix products, arithmetic and copies ran while one was open for 16% -> 6% of each run, Pallas kernels for 0% -> 1%
where the time goes in v1:
time: 896 us; the launch traced here: 894 us
  waiting for transfers between devices  679 us (76%)
  blocking collectives  88.9 us (10%)
  matrix products  43 us (5%)
  local copies, waits for them, and re-layouts  37.1 us (4%)
  Pallas kernels  18.6 us (2%)
  between operations  15.1 us (2%)
  other arithmetic  11.5 us (1%)
    reduce_scatter x3, waiting for transfers between devices, scatter_weight(): lax.psum_scatter(grad.astype(jnp.bfloat16), AXES, scatter_dimension=0, ti...  319 us
    unnamed x12, waiting for transfers between devices  203 us
    all_gather x4, waiting for transfers between devices, gather_all(): return lax.all_gather(array, AXES, axis=0, tiled=True)  134 us
    all_gather x1, blocking collectives, gather_all(): return lax.all_gather(array, AXES, axis=0, tiled=True)  71.2 us
    reduce_scatter x1, waiting for transfers between devices, on_device(): lax.psum_scatter(input_share.astype(jnp.bfloat16), 'ctx', scatter_dimensi...  23.2 us
  transfers between devices with their start and end apart: 10, of which 9 were waited for; matrix products, arithmetic and copies ran while one was open for 6% of the time, Pallas kernels for 1%

profile of v1, /device:TPU:0, one launch (start us, length us, event | category | flops | bytes accessed | tf_op | source)
XLA Modules:
  0.0 894.1 jit_solution(5043611619943172393)
XLA Ops:
  10.0 5.4 concatenate.22
  15.5 71.2 %all_gather.19 = f32[256,128]{1,0:T(8,128)S(1)} all-gather(f32[8,128]{1,0:T(8,128)S(1)} %bitcast_convert_fusion), channel_id=1, replica_groups=mesh['dp'=8,'ctx'=4] {'dp','ctx'}, dimensions={0}, use_global_device_ids=true | all-gather | bytes 135168 | tf_op jit(solution)/shard_map/all_gather | solution.py:159
  88.3 17.7 %all_gather.20 = bf16[512,768]{1,0:T(8,128)(2,1)S(1)} all-gather(bf16[128,768]{1,0:T(8,128)(2,1)} %param.15), channel_id=1, replica_groups=mesh['dp'=8,'ctx'=4] {'ctx'}, dimensions={0}, use_global_device_ids=true | all-gather | bytes 983040 | tf_op jit(solution)/shard_map/all_gather | solution.py:226
  106.0 2.6 fusion.16.query_ref
  108.5 4.2 fusion.key_ref.value_ref
  112.8 7.7 attend_forward.1
  120.5 9.5 %all-gather.7.cloned.1.call-done = bf16[768,768]{1,0:T(8,128)(2,1)} async-done(((bf16[24,768]{1,0:T(8,128)(2,1)}), bf16[768,768]{1,0:T(8,128)(2,1)}) %all-gather.7.cloned.1.call-update) | async-done | bytes 1179664 | tf_op jit(solution)/shard_map/all_gather | solution.py:159
  130.0 1.8 fusion.44
  132.0 63.3 %all-gather.9.cloned.1.call-done = bf16[768,3072]{1,0:T(8,128)(2,1)} async-done(((bf16[24,3072]{1,0:T(8,128)(2,1)}), bf16[768,3072]{1,0:T(8,128)(2,1)}) %all-gather.9.cloned.1.call-update) | async-done | bytes 4718608 | tf_op jit(solution)/shard_map/all_gather | solution.py:159
  195.3 3.2 convolution_add_fusion
  198.6 61.4 %all-gather.11.cloned.1.call-done = bf16[3072,768]{1,0:T(8,128)(2,1)} async-done(((bf16[96,768]{1,0:T(8,128)(2,1)}), bf16[3072,768]{1,0:T(8,128)(2,1)}) %all-gather.11.cloned.1.call-update) | async-done | bytes 4718608 | tf_op jit(solution)/shard_map/all_gather | solution.py:159
  259.9 3.6 fusion.45
  264.5 1.5 fusion.38
  266.0 2.9 fusion.46
  268.9 2.3 multiply_reduce_fusion
  273.8 10.8 %attend_backward.1 = (bf16[128,768]{1,0:T(8,128)(2,1)}, bf16[512,768]{1,0:T(8,128)(2,1)}, bf16[512,768]{1,0:T(8,128)(2,1)}, f32[8,768]{1,0:T(8,128)}, f32[8,768]{1,0:T(8,128)}) custom-call(s32[1]{0:T(128)S(6)} %copy.35.length_ref, bf16[128,768]{1,0:T(8,128)(2,1)} %fusion.16.query_ref, bf16[512,1536]{1,0:T(8,128)(2,1)} %fusion.key_ref.value_ref, ...), custom_call_target="tpu_custom_call" | custom-call | flops 503316480 | bytes 3145728 | tf_op jit(solution)/shard_map/attend_backward/pallas_call | solution.py:139
  284.6 1.3 slice_reduce_fusion.1
  286.7 1.3 slice_reduce_fusion
  288.1 1.4 concatenate.26
  289.4 1.4 reshape.125
  290.8 1.4 reshape.126
  292.1 1.4 reshape.127
  293.5 1.4 reshape.128
  294.9 1.4 reshape.129
  296.2 1.4 reshape.130
  297.6 1.4 reshape.131
  298.9 1.3 pad_maximum_fusion.1
  300.2 1.6 concatenate.28
  301.8 1.5 pad.11
  303.3 1.6 reshape.132
  304.9 2.5 convolution_convert_fusion.2
  307.6 2.4 fusion.14
  310.1 3.0 add_convert_fusion
  313.1 1.6 fusion.9
  316.8 2.1 pad_maximum_fusion
  318.8 5.8 copy.32
  325.3 3.6 convolution_convert_fusion.1
  329.0 3.8 convolution_convert_fusion
  332.9 95.0 %all-reduce.6.cloned.1.call-done = f32[256,128]{1,0:T(8,128)} async-done(((f32[256,128]{1,0:T(8,128)}), f32[256,128]{1,0:T(8,128)}) %all-reduce.6.cloned.1.call-update) | async-done | bytes 131088
  430.2 98.6 %reduce-scatter.10.cloned.1.call-done = bf16[24,768]{1,0:T(8,128)(2,1)} async-done(((bf16[768,768]{1,0:T(8,128)(2,1)}), bf16[24,768]{1,0:T(8,128)(2,1)}) %reduce-scatter.10.cloned.1.call-update) | async-done | bytes 36880 | tf_op jit(solution)/shard_map/reduce_scatter | solution.py:190
  528.9 1.4 convert_element_type.88
  530.3 23.2 %reduce-scatter.8.cloned.1.call-done = bf16[128,768]{1,0:T(8,128)(2,1)} async-done(((bf16[512,768]{1,0:T(8,128)(2,1)}), bf16[128,768]{1,0:T(8,128)(2,1)}) %reduce-scatter.8.cloned.1.call-update) | async-done | bytes 196624 | tf_op jit(solution)/shard_map/reduce_scatter | solution.py:271
  553.5 2.6 fusion.11
  556.0 105.7 %reduce-scatter.16.cloned.1.call-done = bf16[24,2304]{1,0:T(8,128)(2,1)} async-done(((bf16[768,2304]{1,0:T(8,128)(2,1)}), bf16[24,2304]{1,0:T(8,128)(2,1)}) %reduce-scatter.16.cloned.1.call-update) | async-done | bytes 110608
  664.0 109.9 %reduce-scatter.12.cloned.1.call-done = bf16[24,3072]{1,0:T(8,128)(2,1)} async-done(((bf16[768,3072]{1,0:T(8,128)(2,1)}), bf16[24,3072]{1,0:T(8,128)(2,1)}) %reduce-scatter.12.cloned.1.call-update) | async-done | bytes 147472 | tf_op jit(solution)/shard_map/reduce_scatter | solution.py:190
  773.9 1.6 convert_element_type.90
  775.5 110.1 %reduce-scatter.14.cloned.1.call-done = bf16[96,768]{1,0:T(8,128)(2,1)} async-done(((bf16[3072,768]{1,0:T(8,128)(2,1)}), bf16[96,768]{1,0:T(8,128)(2,1)}) %reduce-scatter.14.cloned.1.call-update) | async-done | bytes 147472 | tf_op jit(solution)/shard_map/reduce_scatter | solution.py:190
  885.6 1.6 convert_element_type.92
  (90 shorter events, 15.7 us)
Async XLA Ops:
  7.2 98.8 %copy-start.1 = (bf16[128,768]{1,0:T(8,128)(2,1)S(1)}, bf16[128,768]{1,0:T(8,128)(2,1)}, u32[]{:S(2)}) copy-start(bf16[128,768]{1,0:T(8,128)(2,1)} %param.15) | copy-start | bytes 589828
  7.2 98.8 %all-gather.5.cloned.1.call-start = ((), (), s32[]{:S(2)}) async-start(), calls=%async_computation.5 | async-start | bytes 3649536 | tf_op jit(solution)/shard_map/all_gather | solution.py:159
  7.9 122.0 %all-gather.7.cloned.1.call-start = ((), (), s32[]{:S(2)}) async-start(), calls=%async_computation.6 | async-start | bytes 1216512 | tf_op jit(solution)/shard_map/all_gather | solution.py:159
  8.7 186.7 %all-gather.9.cloned.1.call-start = ((), (), s32[]{:S(2)}) async-start(), calls=%async_computation.7 | async-start | bytes 4866048 | tf_op jit(solution)/shard_map/all_gather | solution.py:159
  9.4 250.5 %all-gather.11.cloned.1.call-start = ((), (), s32[]{:S(2)}) async-start(), calls=%async_computation.8 | async-start | bytes 4866048 | tf_op jit(solution)/shard_map/all_gather | solution.py:159
  10.0 417.9 %all-reduce.6.cloned.1.call-start = ((), (), s32[]{:S(2)}) async-start(), calls=%async_computation.14 | async-start | bytes 262144
  106.0 6.8 copy-start.4
  131.8 139.5 %copy-start.6 = (f32[128]{0:T(128)}, f32[128]{0:T(128)S(1)}, u32[]{:S(2)}) copy-start(f32[128]{0:T(128)S(1)} %broadcast_multiply_fusion.5) | copy-start | bytes 1540
  132.0 139.3 %copy-start.8 = (f32[128]{0:T(128)}, f32[128]{0:T(128)S(1)}, u32[]{:S(2)}) copy-start(f32[128]{0:T(128)S(1)} %add_rsqrt_fusion.1) | copy-start | bytes 1540
  198.5 65.2 %copy-start.3 = (bf16[128,768]{1,0:T(8,128)(2,1)S(1)}, bf16[128,768]{1,0:T(8,128)(2,1)}, u32[]{:S(2)}) copy-start(bf16[128,768]{1,0:T(8,128)(2,1)} %param.29) | copy-start | bytes 589828
  259.9 6.1 copy-start.10
  264.5 4.4 slice-start
  266.0 2.9 slice-start.1
  271.3 1.3 copy-start
  304.9 224.0 %reduce-scatter.10.cloned.1.call-start = ((), (), s32[]{:S(2)}) async-start(), calls=%async_computation.10 | async-start | bytes 1216512 | tf_op jit(solution)/shard_map/reduce_scatter | solution.py:190
  307.4 246.1 %reduce-scatter.8.cloned.1.call-start = ((), (), s32[]{:S(2)}) async-start(), calls=%async_computation.9 | async-start | bytes 983040 | tf_op jit(solution)/shard_map/reduce_scatter | solution.py:271
  307.6 2.4 copy-start.11
  313.1 348.7 %reduce-scatter.16.cloned.1.call-start = ((), (), s32[]{:S(2)}) async-start(), calls=%async_computation.13 | async-start | bytes 3649536
  313.1 1.7 copy-start.5
  313.1 1.7 copy-start.13
  314.8 1.1 copy-start.12
  324.6 0.7 copy-start.7
  324.6 0.7 copy-start.9
  324.7 449.2 %reduce-scatter.12.cloned.1.call-start = ((), (), s32[]{:S(2)}) async-start(), calls=%async_computation.11 | async-start | bytes 4866048 | tf_op jit(solution)/shard_map/reduce_scatter | solution.py:190
  329.0 556.6 %reduce-scatter.14.cloned.1.call-start = ((), (), s32[]{:S(2)}) async-start(), calls=%async_computation.12 | async-start | bytes 4866048 | tf_op jit(solution)/shard_map/reduce_scatter | solution.py:190
  332.8 220.6 %copy-start.2 = (bf16[128,768]{1,0:T(8,128)(2,1)S(1)}, bf16[128,768]{1,0:T(8,128)(2,1)}, u32[]{:S(2)}) copy-start(bf16[128,768]{1,0:T(8,128)(2,1)} %get-tuple-element.19) | copy-start | bytes 589828
Sparse Core Ops, SparseCore 0:
  10.8 63.0 all-gather.4
  76.7 53.1 all-gather.6
  132.8 62.5 all-gather.8
  198.0 61.8 all-gather.10
  305.0 122.8 all-reduce.5
  432.8 96.0 reduce-scatter.9
  531.2 22.2 reduce-scatter.7
  558.9 102.8 reduce-scatter.15
  667.3 106.5 reduce-scatter.11
  779.2 106.3 reduce-scatter.13

commit v2 on v1

--- a/solution.py
+++ b/solution.py
@@ -102,36 +102,36 @@
         )
 
 
-def attention_specs(rows, total, pairs):
+def attention_specs(rows, total):
     local = pl.BlockSpec((rows, LANES), lambda p: (0, p))
     return (
         pl.BlockSpec(memory_space=pltpu.SMEM),
         local,
         pl.BlockSpec((total, LANES), lambda p: (0, p)),
-        pl.BlockSpec((total, LANES), lambda p: (0, pairs + p)),
-    )
-
-
-def attention_forward(lengths, queries, keys_values):
+        pl.BlockSpec((total, LANES), lambda p: (0, p)),
+    )
+
+
+def attention_forward(lengths, queries, keys, values):
     rows, width = queries.shape
-    total, pairs = keys_values.shape[0], width // LANES
+    total, pairs = keys.shape[0], width // LANES
     work = 4 * rows * total * width
     return pl.pallas_call(
         forward_kernel,
         grid=(pairs,),
-        in_specs=attention_specs(rows, total, pairs),
+        in_specs=attention_specs(rows, total),
         out_specs=pl.BlockSpec((rows, LANES), lambda p: (0, p)),
         out_shape=jax.ShapeDtypeStruct((rows, width), jnp.bfloat16),
         cost_estimate=pl.CostEstimate(
             flops=work, bytes_accessed=4 * total * width, transcendentals=work // 64
         ),
         name="attend_forward",
-    )(lengths, queries, keys_values, keys_values)
-
-
-def attention_backward(lengths, queries, keys_values, grad_attended):
+    )(lengths, queries, keys, values)
+
+
+def attention_backward(lengths, queries, keys, values, grad_attended):
     rows, width = queries.shape
-    total, pairs = keys_values.shape[0], width // LANES
+    total, pairs = keys.shape[0], width // LANES
     work = 10 * rows * total * width
     local = pl.BlockSpec((rows, LANES), lambda p: (0, p))
     long = pl.BlockSpec((total, LANES), lambda p: (0, p))
@@ -139,7 +139,7 @@
     return pl.pallas_call(
         backward_kernel,
         grid=(pairs,),
-        in_specs=(*attention_specs(rows, total, pairs), local),
+        in_specs=(*attention_specs(rows, total), local),
         out_specs=(local, long, long, short, short),
         out_shape=(
             jax.ShapeDtypeStruct((rows, width), jnp.bfloat16),
@@ -152,44 +152,64 @@
             flops=work, bytes_accessed=8 * total * width, transcendentals=work // 320
         ),
         name="attend_backward",
-    )(lengths, queries, keys_values, keys_values, grad_attended)
-
-
-def gather_all(array):
-    return lax.all_gather(array, AXES, axis=0, tiled=True)
-
-
-def gather_vectors(vectors):
-    packed = jnp.concatenate([vector.astype(jnp.float32) for vector in vectors])
-    padded = jnp.pad(packed, (0, -packed.shape[0] % (8 * LANES)))
-    every = gather_all(padded.reshape(-1, LANES)).reshape(-1, padded.shape[0])
+    )(lengths, queries, keys, values, grad_attended)
+
+
+def row_blocks(array, width):
+    return [array[:, start : start + width] for start in range(0, array.shape[1], width)]
+
+
+def gather_parameters(weights, vectors, width):
+    packed = jnp.concatenate(vectors)
+    packed = jnp.pad(packed, (0, -packed.shape[0] % width)).reshape(-1, width)
+    rows = jnp.concatenate([b for w in weights for b in row_blocks(w, width)] + [packed], axis=0)
+    rows = jnp.pad(rows, ((0, -rows.shape[0] % 8), (0, 0)))
+    every = lax.all_gather(rows, AXES, axis=0)
+    full, offset = [], 0
+    for weight in weights:
+        blocks = []
+        for _ in range(weight.shape[1] // width):
+            block = every[:, offset : offset + weight.shape[0]]
+            blocks.append(block.reshape(-1, width))
+            offset += weight.shape[0]
+        full.append(blocks)
+    flat = every[:, offset : offset + packed.shape[0]].reshape(every.shape[0], -1)
+    flat = flat.astype(jnp.float32)
     spread, offset = [], 0
     for vector in vectors:
-        spread.append(every[:, offset : offset + vector.shape[0]].reshape(-1))
+        spread.append(flat[:, offset : offset + vector.shape[0]].reshape(-1))
         offset += vector.shape[0]
-    return spread
-
-
-def scatter_vectors(vectors, count):
+    return full, spread
+
+
+def scatter_gradients(weights, vectors, count, width):
+    low = jnp.bfloat16
     sizes = [vector.shape[0] // count for vector in vectors]
     packed = jnp.concatenate(
         [vector.reshape(count, size) for vector, size in zip(vectors, sizes)], axis=1
-    )
-    padded = jnp.pad(packed, ((0, 0), (0, -packed.shape[1] % (8 * LANES))))
+    ).astype(low)
+    packed = jnp.pad(packed, ((0, 0), (0, -packed.shape[1] % width))).reshape(count, -1, width)
+    blocks = [block.astype(low).reshape(count, -1, width) for w in weights for block in w]
+    rows = jnp.concatenate(blocks + [packed], axis=1)
+    rows = jnp.pad(rows, ((0, 0), (0, -rows.shape[1] % 8), (0, 0)))
+    depth = rows.shape[1]
     mine = lax.psum_scatter(
-        padded.reshape(-1, LANES), AXES, scatter_dimension=0, tiled=True
-    ).reshape(-1)
-    pieces, offset = [], 0
+        rows.reshape(count * depth, width), AXES, scatter_dimension=0, tiled=True
+    ).astype(jnp.float32)
+    summed, offset = [], 0
+    for weight in weights:
+        pieces = []
+        for block in weight:
+            owned = block.shape[0] // count
+            pieces.append(mine[offset : offset + owned])
+            offset += owned
+        summed.append(jnp.concatenate(pieces, axis=1))
+    flat = mine[offset : offset + packed.shape[1]].reshape(-1)
+    parts, offset = [], 0
     for size in sizes:
-        pieces.append(mine[offset : offset + size])
+        parts.append(flat[offset : offset + size])
         offset += size
-    return pieces
-
-
-def scatter_weight(grad):
-    return lax.psum_scatter(
-        grad.astype(jnp.bfloat16), AXES, scatter_dimension=0, tiled=True
-    ).astype(jnp.float32)
+    return summed, parts
 
 
 def on_device(
@@ -211,30 +231,29 @@
 ):
     width = layer_input.shape[1]
     count = lax.axis_size("dp") * lax.axis_size("ctx")
+    sequence = lax.all_gather(layer_input, "ctx", axis=0, tiled=True)
     (
-        bias_wide,
-        out_bias_wide,
-        gain_one,
-        shift_one,
-        up_bias_wide,
-        down_bias_wide,
-        gain_two,
-        shift_two,
-    ) = gather_vectors(
-        (qv_bias, out_bias, first_gain, first_shift, up_bias, down_bias, second_gain, second_shift)
-    )
-    sequence = lax.all_gather(layer_input, "ctx", axis=0, tiled=True)
-    full_qkv = gather_all(qkv_weight)
-    full_out = gather_all(out_weight)
-    full_up = gather_all(up_weight)
-    full_down = gather_all(down_weight)
-    weight_q = full_qkv[:, :width]
-    weight_k = full_qkv[:, width : 2 * width]
-    weight_v = full_qkv[:, 2 * width :]
+        ((weight_q, weight_k, weight_v), (full_out,), up_blocks, (full_down,)),
+        (
+            bias_wide,
+            out_bias_wide,
+            gain_one,
+            shift_one,
+            up_bias_wide,
+            down_bias_wide,
+            gain_two,
+            shift_two,
+        ),
+    ) = gather_parameters(
+        (qkv_weight, out_weight, up_weight, down_weight),
+        (qv_bias, out_bias, first_gain, first_shift, up_bias, down_bias, second_gain, second_shift),
+        width,
+    )
+    full_up = jnp.concatenate(up_blocks, axis=1)
     queries = (product(layer_input, weight_q) + bias_wide[:width]).astype(jnp.bfloat16)
-    kv_bias = jnp.concatenate([jnp.zeros((width,), jnp.float32), bias_wide[width:]])
-    keys_values = (product(sequence, full_qkv[:, width:]) + kv_bias).astype(jnp.bfloat16)
-    attended_low = attention_forward(lengths, queries, keys_values)
+    keys = product(sequence, weight_k).astype(jnp.bfloat16)
+    values = (product(sequence, weight_v) + bias_wide[width:]).astype(jnp.bfloat16)
+    attended_low = attention_forward(lengths, queries, keys, values)
     first_sum = layer_input.astype(jnp.float32) + product(attended_low, full_out) + out_bias_wide
     hidden, normed_first, inverse_first = norm_forward(first_sum, gain_one, shift_one)
     hidden_low = hidden.astype(jnp.bfloat16)
@@ -250,48 +269,35 @@
     grad_second = norm_backward(cot_wide, normed_second, inverse_second, gain_two)
     down_bias_grad = jnp.sum(grad_second, axis=0)
     grad_second_low = grad_second.astype(jnp.bfloat16)
-    down_weight_grad = scatter_weight(product_tn(activation_low, grad_second_low))
+    down_weight_grad = product_tn(activation_low, grad_second_low)
     grad_upper = gelu_back(product_nt(grad_second_low, full_down))[0]
     up_bias_grad = jnp.sum(grad_upper, axis=0)
     grad_upper_low = grad_upper.astype(jnp.bfloat16)
-    up_weight_grad = scatter_weight(product_tn(hidden_low, grad_upper_low))
+    up_weight_grad = product_tn(hidden_low, grad_upper_low)
     grad_hidden = grad_second + product_nt(grad_upper_low, full_up)
     first_shift_grad = jnp.sum(grad_hidden, axis=0)
     first_gain_grad = jnp.sum(grad_hidden * normed_first, axis=0)
     grad_first = norm_backward(grad_hidden, normed_first, inverse_first, gain_one)
     out_bias_grad = jnp.sum(grad_first, axis=0)
     grad_first_low = grad_first.astype(jnp.bfloat16)
-    out_weight_grad = scatter_weight(product_tn(attended_low, grad_first_low))
+    out_weight_grad = product_tn(attended_low, grad_first_low)
     grad_attended = product_nt(grad_first_low, full_out).astype(jnp.bfloat16)
     grad_queries, grad_keys, grad_values, query_sums, value_sums = attention_backward(
-        lengths, queries, keys_values, grad_attended
+        lengths, queries, keys, values, grad_attended
     )
     qv_bias_grad = jnp.concatenate([query_sums[0], value_sums[0]])
     input_share = product_nt(grad_keys, weight_k) + product_nt(grad_values, weight_v)
     others = lax.psum_scatter(
         input_share.astype(jnp.bfloat16), "ctx", scatter_dimension=0, tiled=True
     ).astype(jnp.float32)
-    qkv_weight_grad = scatter_weight(
-        jnp.concatenate(
-            [
-                product_tn(layer_input, grad_queries),
-                product_tn(sequence, grad_keys),
-                product_tn(sequence, grad_values),
-            ],
-            axis=1,
-        )
+    qkv_blocks = (
+        product_tn(layer_input, grad_queries),
+        product_tn(sequence, grad_keys),
+        product_tn(sequence, grad_values),
     )
     input_grad = grad_first + product_nt(grad_queries, weight_q) + others
     (
-        qv_bias_grad,
-        out_bias_grad,
-        first_gain_grad,
-        first_shift_grad,
-        up_bias_grad,
-        down_bias_grad,
-        second_gain_grad,
-        second_shift_grad,
-    ) = scatter_vectors(
+        (qkv_weight_grad, out_weight_grad, up_weight_grad, down_weight_grad),
         (
             qv_bias_grad,
             out_bias_grad,
@@ -302,7 +308,25 @@
             second_gain_grad,
             second_shift_grad,
         ),
+    ) = scatter_gradients(
+        (
+            qkv_blocks,
+            (out_weight_grad,),
+            row_blocks(up_weight_grad, width),
+            (down_weight_grad,),
+        ),
+        (
+            qv_bias_grad,
+            out_bias_grad,
+            first_gain_grad,
+            first_shift_grad,
+            up_bias_grad,
+            down_bias_grad,
+            second_gain_grad,
+            second_shift_grad,
+        ),
         count,
+        width,
     )
     return (
         layer_output,

time: 896 us -> 420 us (0.47)
  waiting for transfers between devices: 679 us -> 245 us
  blocking collectives: 88.9 us -> 27.5 us
  local copies, waits for them, and re-layouts: 37.1 us -> 66.5 us
    unnamed x12 -> x3, waiting for transfers between devices: 203 us -> 0.05 us
    reduce_scatter x3 -> x1, waiting for transfers between devices: 319 us -> 162 us  [scatter_gradients(): lax.psum_scatter(rows.reshape(count * depth, width), AXES, scatter_dimens...]
    all_gather x1 -> x0, blocking collectives: 71.2 us -> none  [gather_all(): return lax.all_gather(array, AXES, axis=0, tiled=True)]
    all_gather x4 -> x1, waiting for transfers between devices: 134 us -> 83.2 us  [gather_parameters(): every = lax.all_gather(rows, AXES, axis=0)]
    reduce_scatter x1, waiting for transfers between devices: 23.2 us -> 0.02 us  [on_device(): lax.psum_scatter(input_share.astype(jnp.bfloat16), 'ctx', scatter_dimensi...]
    slice x5 -> x11, local copies, waits for them, and re-layouts: 1.85 us -> 20.5 us  [the longest x2 11.3 us: gather_parameters(): block = every[:, offset:offset + weight.shape[0]]]
    unnamed x35 -> x98, local copies, waits for them, and re-layouts: 9.42 us -> 23.1 us
    reshape x10 -> x8, local copies, waits for them, and re-layouts: 11.8 us -> 1.25 us  [the longest x7 1.24 us: scatter_gradients(): vector.reshape(count, size)]
  transfers between devices with their start and end apart: 10 -> 3, of which waited for: 9 -> 2; matrix products, arithmetic and copies ran while one was open for 6% -> 9% of each run, Pallas kernels for 1% -> 0%
where the time goes in v2:
time: 420 us; the launch traced here: 419 us
  waiting for transfers between devices  245 us (58%)
  local copies, waits for them, and re-layouts  66.5 us (16%)
  matrix products  38.1 us (9%)
  blocking collectives  27.5 us (7%)
  Pallas kernels  18.6 us (4%)
  between operations  15 us (4%)
  other arithmetic  7.51 us (2%)
    reduce_scatter x1, waiting for transfers between devices, scatter_gradients(): lax.psum_scatter(rows.reshape(count * depth, width), AXES, scatter_dimens...  162 us
    all_gather x1, waiting for transfers between devices, gather_parameters(): every = lax.all_gather(rows, AXES, axis=0)  83.2 us
    all_gather x1, blocking collectives, on_device(): sequence = lax.all_gather(layer_input, 'ctx', axis=0, tiled=True)  27.5 us
    unnamed x98, local copies, waits for them, and re-layouts  23.1 us
    dot_general x6, matrix products, product_nt(): lax.dot_general(left, right, (((1,), (1,)), ((), ())), preferred_element_...  13.8 us
    dot_general x6, matrix products, product(): return jnp.dot(left, right, preferred_element_type=jnp.float32)  13.2 us
    slice x2, local copies, waits for them, and re-layouts, gather_parameters(): block = every[:, offset:offset + weight.shape[0]]  11.3 us
    dot_general x6, matrix products, product_tn(): lax.dot_general(left, right, (((0,), (0,)), ((), ())), preferred_element_...  11 us
  transfers between devices with their start and end apart: 3, of which 2 were waited for; matrix products, arithmetic and copies ran while one was open for 9% of the time, Pallas kernels for 0%

profile of v2, /device:TPU:0, one launch (start us, length us, event | category | flops | bytes accessed | tf_op | source)
XLA Modules:
  0.0 418.6 jit_solution(16615493482375804516)
XLA Ops:
  7.2 0.9 constant_dynamic-update-slice_fusion.9
  8.1 0.8 constant_dynamic-update-slice_fusion.8
  8.9 0.8 constant_dynamic-update-slice_fusion.7
  12.0 0.8 constant_dynamic-update-slice_fusion.3
  13.5 0.9 constant_dynamic-update-slice_fusion.1
  14.4 5.4 %concatenate.31 = bf16[288]{0:T(512)(128)(2,1)S(1)} concatenate(bf16[48]{0:T(256)(128)(2,1)} %param.18, bf16[24]{0:T(256)(128)(2,1)} %param.20, bf16[24]{0:T(256)(128)(2,1)} %param.21, bf16[24]{0:T(256)(128)(2,1)} %param.22, bf16[96]{0:T(256)(128)(2,1)} %param.24, bf16[24]{0:T(256)(128)(2,1)} %param.26, bf16[24]{0:T(256)(128)(2,1)} %param.27, bf16[24]{0:T(256)(128)(2,1)} %param.28), dimensions={0} | concatenate | bytes 1152 | tf_op jit(solution)/shard_map/concatenate | solution.py:163
  19.9 0.8 pad.17
  22.2 27.5 %all_gather.11 = bf16[512,768]{1,0:T(8,128)(2,1)} all-gather(bf16[128,768]{1,0:T(8,128)(2,1)S(1)} %copy-done.7), channel_id=1, replica_groups=mesh['dp'=8,'ctx'=4] {'ctx'}, dimensions={0}, use_global_device_ids=true | all-gather | bytes 983040 | tf_op jit(solution)/shard_map/all_gather | solution.py:234
  49.6 83.2 %all-gather.3.cloned.1.call-done = bf16[9472,768]{1,0:T(8,128)(2,1)} async-done(((bf16[296,768]{1,0:T(8,128)(2,1)}), bf16[9472,768]{1,0:T(8,128)(2,1)}) %all-gather.3.cloned.1.call-update) | async-done | bytes 14549008 | tf_op jit(solution)/shard_map/all_gather | solution.py:167
  132.8 1.0 slice.249
  133.9 4.8 %slice.263 = bf16[32,96,768]{2,1,0:T(8,128)(2,1)} slice(bf16[32,296,768]{2,1,0:T(8,128)(2,1)} %bitcast.84), slice={[0:32], [192:288], [0:768]} | slice | bytes 9437184 | tf_op jit(solution)/shard_map/slice | solution.py:172
  138.7 6.5 %fusion.39 = (bf16[32,24,768]{2,1,0:T(8,128)(2,1)}, bf16[32,24,768]{2,1,0:T(8,128)(2,1)}, bf16[32,24,768]{2,1,0:T(8,128)(2,1)}, bf16[32,24,768]{2,1,0:T(8,128)(2...) fusion(bf16[32,296,768]{2,1,0:T(8,128)(2,1)} %bitcast.85), kind=kLoop, calls=%fused_computation.111 | loop fusion | bytes 18874368 | tf_op jit(solution)/shard_map/slice | solution.py:172
  146.6 1.0 fusion.11.query_ref
  147.8 3.0 fusion.6.key_ref
  150.8 1.7 fusion.5.value_ref
  152.5 7.7 %attend_forward.1 = bf16[128,768]{1,0:T(8,128)(2,1)} custom-call(s32[1]{0:T(128)S(6)} %copy.63.length_ref, bf16[128,768]{1,0:T(8,128)(2,1)} %fusion.11.query_ref, bf16[512,768]{1,0:T(8,128)(2,1)} %fusion.6.key_ref, bf16[512,768]{1,0:T(8,128)(2,1)} %fusion.5.value_ref), custom_call_target="tpu_custom_call" | custom-call | flops 201326592 | bytes 1572864 | tf_op jit(solution)/shard_map/attend_forward/pallas_call | solution.py:119
  160.1 1.5 fusion.44
  161.9 5.0 %convolution_add_fusion = f32[128,3072]{1,0:T(8,128)S(1)} fusion(bf16[768,768]{1,0:T(8,128)(2,1)S(1)} %bitcast.106, bf16[768,768]{1,0:T(8,128)(2,1)} %bitcast.108, bf16[768,768]{1,0:T(8,128)(2,1)} %bitcast.110, bf16[768,768]{1,0:T(8,128)(2,1)S(1)} %bitcast.104, f32[3072]{0:T(1024)S(1)} %add.139, f32[128,768]{1,0:T(8,128)S(1)} %get-tuple-element.71, ...), kind=kOutput, calls=%fused_computation.3 | convolution fusion | flops 623738880 | bytes 6704128 | tf_op jit(solution)/shard_map/dot_general | solution.py:23
  166.9 1.1 fusion.45
  168.8 0.8 mul.160
  169.6 0.8 add.149
  170.4 1.6 fusion.18
  172.1 2.1 fusion.36
  174.2 4.8 %fusion.46 = (bf16[3072]{0:T(1024)(128)(2,1)S(1)}, bf16[128,3072]{1,0:T(8,128)(2,1)S(1)}) fusion(f32[128,3072]{1,0:T(8,128)S(1)} %copy-done.1, bf16[3072,768]{1,0:T(8,128)(2,1)} %bitcast.94, f32[128,768]{1,0:T(8,128)S(1)} %get-tuple-element.32), kind=kOutput, calls=%fused_computation.118 | convolution fusion | flops 613905408 | bytes 7477248 | tf_op jit(solution)/shard_map/dot_general | solution.py:33
  179.2 1.8 multiply_reduce_fusion
  181.2 1.2 convolution_convert_fusion.7.grad_ref
  182.4 10.9 %attend_backward.1 = (bf16[128,768]{1,0:T(8,128)(2,1)}, bf16[512,768]{1,0:T(8,128)(2,1)}, bf16[512,768]{1,0:T(8,128)(2,1)}, f32[8,768]{1,0:T(8,128)}, f32[8,768]{1,0:T(8,128)}) custom-call(s32[1]{0:T(128)S(6)} %copy.63.length_ref, bf16[128,768]{1,0:T(8,128)(2,1)} %fusion.11.query_ref, bf16[512,768]{1,0:T(8,128)(2,1)} %fusion.6.key_ref, ...), custom_call_target="tpu_custom_call" | custom-call | flops 503316480 | bytes 3145728 | tf_op jit(solution)/shard_map/attend_backward/pallas_call | solution.py:139
  193.3 2.1 fusion.47
  195.4 1.9 convolution_convert_fusion.4
  197.3 1.6 convolution_convert_fusion.2
  198.9 3.6 convolution_convert_fusion.1
  202.5 1.8 convolution_convert_fusion.3
  204.3 1.7 add_convert_fusion
  206.7 1.1 constant_dynamic-update-slice_fusion.18
  207.8 4.3 %fusion.40 = (bf16[768,768]{1,0:T(8,128)(2,1)}, bf16[768,768]{1,0:T(8,128)(2,1)S(1)}, bf16[768,768]{1,0:T(8,128)(2,1)}, bf16[768,768]{1,0:T(8,128)(2,1)}) fusion(bf16[768,3072]{1,0:T(8,128)(2,1)} %convolution_convert_fusion.1), kind=kLoop, calls=%fused_computation.112 | loop fusion | bytes 9437184 | tf_op jit(solution)/shard_map/slice | solution.py:159
  214.4 2.5 constant_dynamic-update-slice_fusion.17
  216.9 1.1 constant_dynamic-update-slice_fusion.16
  218.2 2.5 constant_dynamic-update-slice_fusion.15
  220.7 1.2 constant_dynamic-update-slice_fusion.14
  222.4 1.1 constant_dynamic-update-slice_fusion.13
  223.5 1.1 constant_dynamic-update-slice_fusion.12
  225.2 1.2 constant_dynamic-update-slice_fusion.11
  226.4 1.6 convolution_convert_fusion
  228.1 2.5 constant_dynamic-update-slice_fusion.10
  231.4 10.7 %pad.19 = bf16[32,296,768]{2,1,0:T(8,128)(2,1)} pad(bf16[32,289,768]{2,1,0:T(8,128)(2,1)} %copy_dynamic-update-slice_fusion, bf16[]{:T(256)} %constant.17.clone.1), padding=0_0x0_7x0_0 | pad | bytes 28753922 | tf_op jit(solution)/shard_map/jit(_pad)/pad | solution.py:194
  242.1 2.2 fusion.8
  244.3 162.1 %reduce-scatter.5.cloned.1.call-done = bf16[296,768]{1,0:T(8,128)(2,1)} async-done(((bf16[9472,768]{1,0:T(8,128)(2,1)}), bf16[296,768]{1,0:T(8,128)(2,1)}) %reduce-scatter.5.cloned.1.call-update) | async-done | bytes 454672 | tf_op jit(solution)/shard_map/reduce_scatter | solution.py:196
  406.4 1.1 convert_element_type.121
  (139 shorter events, 16.1 us)
Async XLA Ops:
  7.2 14.3 %copy-start.8 = (bf16[128,768]{1,0:T(8,128)(2,1)S(1)}, bf16[128,768]{1,0:T(8,128)(2,1)}, u32[]{:S(2)}) copy-start(bf16[128,768]{1,0:T(8,128)(2,1)} %param.29) | copy-start | bytes 589828
  7.2 15.0 %copy-start.7 = (bf16[128,768]{1,0:T(8,128)(2,1)S(1)}, bf16[128,768]{1,0:T(8,128)(2,1)}, u32[]{:S(2)}) copy-start(bf16[128,768]{1,0:T(8,128)(2,1)} %param.15) | copy-start | bytes 589828
  7.2 125.6 %all-gather.3.cloned.1.call-start = ((), (), s32[]{:S(2)}) async-start(), calls=%async_computation.4 | async-start | bytes 15003648 | tf_op jit(solution)/shard_map/all_gather | solution.py:167
  20.7 221.3 %reduce-scatter.3.cloned.1.call-start = ((), (), s32[]{:S(2)}) async-start(), calls=%async_computation.2 | async-start | bytes 983040 | tf_op jit(solution)/shard_map/reduce_scatter | solution.py:290
  146.6 1.3 copy-start.13
  147.8 3.0 copy-start.11
  147.8 3.0 copy-start.26
  160.1 1.7 copy-start.15
  160.1 1.8 copy-start.17
  160.1 6.8 %slice-start = ((s8[4718592]{0:T(1024)(128)(4,1)}), s8[4194304]{0:T(1024)(128)(4,1)S(1)}, s32[]{:S(2)}) async-start(s8[4718592]{0:T(1024)(128)(4,1)} %bitcast.95), calls=%async_computation.5 | async-start | bytes 8388608
  161.6 5.2 %copy-start.29 = (f32[128]{0:T(128)}, f32[128]{0:T(128)S(1)}, u32[]{:S(2)}) copy-start(f32[128]{0:T(128)S(1)} %broadcast_multiply_fusion.5) | copy-start | bytes 1540
  161.9 5.0 %copy-start.33 = (f32[128]{0:T(128)}, f32[128]{0:T(128)S(1)}, u32[]{:S(2)}) copy-start(f32[128]{0:T(128)S(1)} %add_rsqrt_fusion.1) | copy-start | bytes 1540
  161.9 5.0 %slice-start.1 = ((s8[4718592]{0:T(1024)(128)(4,1)}), s8[524288]{0:T(1024)(128)(4,1)S(1)}, s32[]{:S(2)}) async-start(s8[4718592]{0:T(1024)(128)(4,1)} %bitcast.95), calls=%async_computation.6 | async-start | bytes 1048576
  166.9 1.2 copy-start
  168.1 0.7 copy-start.35
  170.4 3.8 copy-start.1
  174.2 4.9 %copy-start.9 = (f32[128,768]{1,0:T(8,128)}, f32[128,768]{1,0:T(8,128)S(1)}, u32[]{:S(2)}) copy-start(f32[128,768]{1,0:T(8,128)S(1)} %get-tuple-element.32) | copy-start | bytes 1179652
  174.2 4.9 %copy-start.16 = (bf16[32,24,768]{2,1,0:T(8,128)(2,1)S(1)}, bf16[32,24,768]{2,1,0:T(8,128)(2,1)}, u32[]{:S(2)}) copy-start(bf16[32,24,768]{2,1,0:T(8,128)(2,1)} %get-tuple-element.35) | copy-start | bytes 3538948
  174.2 4.9 %copy-start.18 = (bf16[32,24,768]{2,1,0:T(8,128)(2,1)S(1)}, bf16[32,24,768]{2,1,0:T(8,128)(2,1)}, u32[]{:S(2)}) copy-start(bf16[32,24,768]{2,1,0:T(8,128)(2,1)} %get-tuple-element.36) | copy-start | bytes 3538948
  174.2 4.9 %copy-start.19 = (bf16[32,24,768]{2,1,0:T(8,128)(2,1)S(1)}, bf16[32,24,768]{2,1,0:T(8,128)(2,1)}, u32[]{:S(2)}) copy-start(bf16[32,24,768]{2,1,0:T(8,128)(2,1)} %get-tuple-element.37) | copy-start | bytes 3538948
  174.2 4.9 %copy-start.20 = (bf16[32,24,768]{2,1,0:T(8,128)(2,1)S(1)}, bf16[32,24,768]{2,1,0:T(8,128)(2,1)}, u32[]{:S(2)}) copy-start(bf16[32,24,768]{2,1,0:T(8,128)(2,1)} %get-tuple-element.38) | copy-start | bytes 3538948
  174.2 4.9 %copy-start.30 = (f32[128]{0:T(128)S(1)}, f32[128]{0:T(128)}, u32[]{:S(2)}) copy-start(f32[128]{0:T(128)} %copy-done.29) | copy-start | bytes 1540
  174.2 4.9 %copy-start.34 = (f32[128]{0:T(128)S(1)}, f32[128]{0:T(128)}, u32[]{:S(2)}) copy-start(f32[128]{0:T(128)} %copy-done.33) | copy-start | bytes 1540
  179.1 1.9 copy-start.22
  182.4 10.9 %copy-start.14 = (bf16[32,24,768]{2,1,0:T(8,128)(2,1)S(1)}, bf16[32,24,768]{2,1,0:T(8,128)(2,1)}, u32[]{:S(2)}) copy-start(bf16[32,24,768]{2,1,0:T(8,128)(2,1)} %get-tuple-element.41) | copy-start | bytes 3538948
  193.3 2.1 copy-start.27
  193.3 2.1 copy-start.37
  195.4 1.9 copy-start.25
  197.3 1.6 copy-start.23
  198.9 3.6 copy-start.36
  202.5 1.8 copy-start.12
  204.3 1.8 copy-start.24
  206.1 200.3 %reduce-scatter.5.cloned.1.call-start = ((), (), s32[]{:S(2)}) async-start(), calls=%async_computation.3 | async-start | bytes 15003648 | tf_op jit(solution)/shard_map/reduce_scatter | solution.py:196
  207.8 6.4 %copy-start.32 = (bf16[768]{0:T(1024)(128)(2,1)S(1)}, bf16[768]{0:T(1024)(128)(2,1)}, u32[]{:S(2)}) copy-start(bf16[768]{0:T(1024)(128)(2,1)} %get-tuple-element.31) | copy-start | bytes 4612
  207.8 6.5 %copy-start.31 = (bf16[768]{0:T(1024)(128)(2,1)S(1)}, bf16[768]{0:T(1024)(128)(2,1)}, u32[]{:S(2)}) copy-start(bf16[768]{0:T(1024)(128)(2,1)} %get-tuple-element.26) | copy-start | bytes 4612
  214.4 2.5 copy-start.21
  216.9 1.1 copy-start.28
  218.2 2.5 copy-start.5
  220.7 1.7 copy-start.4
  223.5 1.7 copy-start.3
  224.7 1.8 copy-start.2
  224.7 1.8 copy-start.10
  406.4 2.9 copy-start.6
Sparse Core Ops, SparseCore 0:
  20.9 111.9 all-gather.2
  206.2 21.5 reduce-scatter.2
  242.2 164.1 reduce-scatter.4
